TPU v7x, 256 devices: a whole 4x4x8 slice. The times are simulated.
256 devices in a mesh: dp: 4 (over y), tensor: 16 (over x_hi, z), rep: 4 (over x_lo, core).
Axes of the slice: x: 4 (x_hi: 2, x_lo: 2; x = x_hi * 2 + x_lo), y: 4, z: 8, core: 2. Of those that a mesh axis runs over, the one named last changes fastest.
Arguments:
- resid: bfloat16 [512, 8192], P('dp', 'rep'), may hold values from -94 to 94
- norm_gain: float32 [8192], P('rep'), may hold values from 0.25 to 1.75
- gate_weight: bfloat16 [4, 2048, 14336], P('rep', 'dp', 'tensor'), may hold values from -0.0625 to 0.0625
- up_weight: bfloat16 [4, 2048, 14336], P('rep', 'dp', 'tensor'), may hold values from -0.0625 to 0.0625
- down_weight: bfloat16 [14336, 4, 2048], P('tensor', 'rep', 'dp'), may hold values from -0.046875 to 0.046875
- enc_weight: bfloat16 [8192, 65536], P('rep', ('dp', 'tensor')), may hold values from -0.0625 to 0.0625
- enc_bias: float32 [65536], P(('dp', 'tensor')), may hold values from -3 to 3
- dec_weight: bfloat16 [65536, 8192], P(('dp', 'tensor'), 'rep'), may hold values from -1 to 1
- dec_bias: float32 [8192], P('rep'), may hold values from -3 to 3
- latent_ids: int32 [512, 64], replicated, may hold values from 0 to 65535, as said below
Outputs:
- resid_out: bfloat16 [512, 8192], P(('dp', 'tensor'), 'rep')
- recon: bfloat16 [512, 8192], P(('dp', 'tensor'), 'rep')
- error_ratio: float32 [512], P(('dp', 'tensor'))
Inputs may be any that keep to these rules, and one draw needn't show every extreme that they name: `latent_ids`: each row names 64 distinct latents: 8 latents in each of 8 distinct blocks of 128 consecutive latents (block b holds latents b * 128 to b * 128 + 127).
All inputs are finite; a program needn't handle non-finite values.
Results may differ from a plain program's by a relative error of at most 0.009.
Values may be sent and summed in bfloat16 or wider, within the bound.
No kernel may reach another device: no remote copies, remote signals or barrier semaphores. Data moves between devices by JAX's collectives and lax.ppermute only.
A program may use at most 64 MiB of HBM per device.

v0:
```python
import jax
import jax.numpy as jnp
from jax import lax
from jax.sharding import PartitionSpec as P


def place_mask(latent_ids, length, slab_first, slab_width):
    slots = latent_ids - slab_first
    inside = (slots >= 0) & (slots < slab_width)
    local_slot = jnp.where(inside, slots, slab_width)
    row_number = lax.broadcasted_iota(jnp.int32, slots.shape, 0)
    return (
        jnp.zeros((length, slab_width), jnp.bool_).at[row_number, local_slot].set(True, mode="drop")
    )


def body(
    resid,
    norm_gain,
    gate_weight,
    up_weight,
    down_weight,
    enc_weight,
    enc_bias,
    dec_weight,
    dec_bias,
    latent_ids,
):
    tok_grp, width_rep = resid.shape
    n_tensor = lax.axis_size("tensor")
    n_rep = lax.axis_size("rep")
    resid_f = resid.astype(jnp.float32)
    squares = lax.psum(jnp.sum(resid_f * resid_f, axis=1), "rep")
    inverse_rms = lax.rsqrt(squares / (width_rep * n_rep) + 1e-05)
    normed = (resid_f * inverse_rms[:, None] * norm_gain[None, :]).astype(jnp.bfloat16)
    gate_part = jnp.dot(
        normed,
        lax.all_gather(gate_weight, "dp", axis=1, tiled=True)[0],
        preferred_element_type=jnp.float32,
    )
    up_part = jnp.dot(
        normed,
        lax.all_gather(up_weight, "dp", axis=1, tiled=True)[0],
        preferred_element_type=jnp.float32,
    )
    gate_pre, up_pre = lax.psum((gate_part, up_part), "rep")
    hidden = (jax.nn.silu(gate_pre) * up_pre).astype(jnp.bfloat16)
    down_terms = jnp.dot(
        hidden,
        lax.all_gather(down_weight, "dp", axis=2, tiled=True)[:, 0, :],
        preferred_element_type=jnp.float32,
    )
    rows_dev = tok_grp // n_tensor
    block_sum = lax.psum(down_terms, "tensor")
    group_out = (resid_f + block_sum).astype(jnp.bfloat16)
    resid_rows = lax.dynamic_slice_in_dim(
        group_out, lax.axis_index("tensor") * rows_dev, rows_dev, 0
    )
    slab_input = lax.all_gather(group_out, "dp", axis=0, tiled=True)
    slab_width = enc_weight.shape[1]
    centred = (slab_input.astype(jnp.float32) - dec_bias[None, :]).astype(jnp.bfloat16)
    slab_first = (lax.axis_index("dp") * n_tensor + lax.axis_index("tensor")) * slab_width
    preact = lax.psum(jnp.dot(centred, enc_weight, preferred_element_type=jnp.float32), "rep")
    length = preact.shape[0]
    chosen = place_mask(latent_ids, length, slab_first, slab_width)
    actives = jnp.where(chosen, jnp.maximum(preact + enc_bias[None, :], 0.0), 0.0).astype(
        jnp.bfloat16
    )
    decoded = (
        lax.psum_scatter(
            jnp.dot(actives, dec_weight, preferred_element_type=jnp.float32),
            ("dp", "tensor"),
            scatter_dimension=0,
            tiled=True,
        )
        + dec_bias[None, :]
    )
    kept_f = resid_rows.astype(jnp.float32)
    misfit = kept_f - decoded
    miss_sum, energy = lax.psum(
        (jnp.sum(misfit * misfit, axis=1), jnp.sum(kept_f * kept_f, axis=1)), "rep"
    )
    error_ratio = miss_sum / (energy + 1e-06)
    return (resid_rows, decoded.astype(jnp.bfloat16), error_ratio)


def solution(mesh):
    in_specs = (
        P("dp", "rep"),
        P("rep"),
        P("rep", "dp", "tensor"),
        P("rep", "dp", "tensor"),
        P("tensor", "rep", "dp"),
        P("rep", ("dp", "tensor")),
        P(("dp", "tensor")),
        P(("dp", "tensor"), "rep"),
        P("rep"),
        P(),
    )
    out_specs = (P(("dp", "tensor"), "rep"), P(("dp", "tensor"), "rep"), P(("dp", "tensor")))
    return jax.shard_map(body, mesh=mesh, in_specs=in_specs, out_specs=out_specs, check_vma=False)
```

profile of v0, /device:TPU:1, one launch (start us, length us, event | category | flops | bytes accessed | tf_op | source)
XLA Modules:
  0.0 939.6 jit_solution(7741894260135573512)
XLA Ops:
  7.2 0.7 all-gather.7.cloned.1.call-update
  8.0 0.7 all-gather.5.cloned.1.call-update
  8.7 0.7 all-gather.9.cloned.1.call-update
  9.5 1.2 fusion.8
  10.7 8.3 psum.49
  18.9 41.2 %all-gather.7.cloned.1.call-done = bf16[1,2048,896]{2,1,0:T(8,128)(2,1)} async-done(((bf16[1,512,896]{2,1,0:T(8,128)(2,1)}), bf16[1,2048,896]{2,1,0:T(8,128)(2,1)}) %all-gather.7.cloned.1.call-update) | async-done | bytes 3670032 | tf_op jit(solution)/shard_map/all_gather | solution.py:43
  60.1 3.8 fusion.2
  63.9 44.8 %all-gather.5.cloned.1.call-done = bf16[1,2048,896]{2,1,0:T(8,128)(2,1)} async-done(((bf16[1,512,896]{2,1,0:T(8,128)(2,1)}), bf16[1,2048,896]{2,1,0:T(8,128)(2,1)}) %all-gather.5.cloned.1.call-update) | async-done | bytes 3670032 | tf_op jit(solution)/shard_map/all_gather | solution.py:38
  108.7 3.6 fusion.4
  112.4 44.9 %all-gather.9.cloned.1.call-done = bf16[896,1,2048]{2,0,1:T(8,128)(2,1)} async-done(((bf16[896,1,512]{2,0,1:T(8,128)(2,1)}), bf16[896,1,2048]{2,0,1:T(8,128)(2,1)}) %all-gather.9.cloned.1.call-update) | async-done | bytes 3670032 | tf_op jit(solution)/shard_map/all_gather | solution.py:50
  157.3 48.5 %all-reduce.10.cloned.1.call-done = (f32[128,896]{1,0:T(8,128)}, f32[128,896]{1,0:T(8,128)}) async-done(((f32[128,896]{1,0:T(8,128)}, f32[128,896]{1,0:T(8,128)}), (f32[128,896]{1,0:T(8,128)}, f32[128,896]{1,0:T(8,128)})) %all-reduce.10.cloned.1.call-update) | async-done | bytes 917520 | tf_op jit(solution)/shard_map/psum | solution.py:46
  205.8 4.0 fusion
  210.0 149.3 %all-reduce.6.cloned.1.call-done = f32[128,2048]{1,0:T(8,128)} async-done(((f32[128,2048]{1,0:T(8,128)}), f32[128,2048]{1,0:T(8,128)}) %all-reduce.6.cloned.1.call-update) | async-done | bytes 1048592 | tf_op jit(solution)/shard_map/psum | solution.py:54
  359.2 2.1 fusion.11
  361.5 41.0 %all-gather.11.cloned.1.call-done = bf16[512,2048]{1,0:T(8,128)(2,1)} async-done(((bf16[128,2048]{1,0:T(8,128)(2,1)}), bf16[512,2048]{1,0:T(8,128)(2,1)}) %all-gather.11.cloned.1.call-update) | async-done | bytes 2097168 | tf_op jit(solution)/shard_map/all_gather | solution.py:59
  402.4 6.5 fusion.6
  409.4 0.1 copy.13
  409.6 137.1 %scatter_custom_fusion = pred[524288]{0:T(1024)(128)(4,1)S(1)} fusion(s32[32768]{0:T(1024)S(1)} %reshape.26, pred[32768]{0:T(1024)(128)(4,1)S(1)} %broadcast.49, pred[]{:T(512)} %constant.14.clone.1), kind=kCustom, calls=%fused_computation.21 | custom fusion | bytes 524289
  546.7 0.6 reshape.25
  547.4 7.1 fusion.12
  554.5 321.2 %reduce-scatter.2.cloned.1.call-done = f32[8,2048]{1,0:T(8,128)} async-done(((f32[512,2048]{1,0:T(8,128)}), f32[8,2048]{1,0:T(8,128)}) %reduce-scatter.2.cloned.1.call-update) | async-done | bytes 65552 | tf_op jit(solution)/shard_map/reduce_scatter | solution.py:70
  875.7 1.6 fusion.23
  877.3 54.9 %all-reduce = (f32[8]{0:T(128)S(1)}, f32[8]{0:T(128)S(1)}) all-reduce(f32[8]{0:T(128)S(1)} %get-tuple-element.4, f32[8]{0:T(128)S(1)} %get-tuple-element.3), channel_id=1, replica_groups=mesh['dp'=4,'tensor'=16,'rep'=4] {'rep'}, use_global_device_ids=true, to_apply=%region_9.10 | all-reduce | flops 16 | bytes 128 | tf_op jit(solution)/shard_map/psum | solution.py:80
  932.2 0.5 add_divide_fusion
  (36 shorter events, 0.9 us)
Async XLA Ops:
  7.2 53.0 %all-gather.7.cloned.1.call-start = ((), (), s32[]{:S(2)}) async-start(), calls=%async_computation.2 | async-start | bytes 4587520 | tf_op jit(solution)/shard_map/all_gather | solution.py:43
  7.9 100.8 %copy-start = (bf16[128,2048]{1,0:T(8,128)(2,1)S(1)}, bf16[128,2048]{1,0:T(8,128)(2,1)}, u32[]{:S(2)}) copy-start(bf16[128,2048]{1,0:T(8,128)(2,1)} %param.10) | copy-start | bytes 1572868
  7.9 100.8 %copy-start.2 = (f32[2048]{0:T(1024)S(1)}, f32[2048]{0:T(1024)}, u32[]{:S(2)}) copy-start(f32[2048]{0:T(1024)} %param.11) | copy-start | bytes 24580
  7.9 100.8 %all-gather.5.cloned.1.call-start = ((), (), s32[]{:S(2)}) async-start(), calls=%async_computation.1 | async-start | bytes 4587520 | tf_op jit(solution)/shard_map/all_gather | solution.py:38
  8.7 148.6 %all-gather.9.cloned.1.call-start = ((), (), s32[]{:S(2)}) async-start(), calls=%async_computation.3 | async-start | bytes 4587520 | tf_op jit(solution)/shard_map/all_gather | solution.py:50
  9.4 196.4 %all-reduce.10.cloned.1.call-start = ((), (), s32[]{:S(2)}) async-start(), calls=%async_computation.8 | async-start | bytes 1835008 | tf_op jit(solution)/shard_map/psum | solution.py:46
  112.3 246.9 %all-reduce.6.cloned.1.call-start = ((), (), s32[]{:S(2)}) async-start(), calls=%async_computation.4 | async-start | bytes 2097152 | tf_op jit(solution)/shard_map/psum | solution.py:54
  205.8 196.6 %copy-start.3 = (f32[2048]{0:T(1024)S(1)}, f32[2048]{0:T(1024)}, u32[]{:S(2)}) copy-start(f32[2048]{0:T(1024)} %param.18) | copy-start | bytes 24580
  209.9 192.5 %all-gather.11.cloned.1.call-start = ((), (), s32[]{:S(2)}) async-start(), calls=%async_computation.5 | async-start | bytes 2621440 | tf_op jit(solution)/shard_map/all_gather | solution.py:59
  361.4 47.7 %copy-start.1 = (s32[512,64]{0,1:T(8,128)S(1)}, s32[512,64]{0,1:T(8,128)}, u32[]{:S(2)}) copy-start(s32[512,64]{0,1:T(8,128)} %param.19) | copy-start | bytes 393220
  361.4 47.7 %copy-start.5 = (s32[2]{0:T(128)S(1)}, s32[2]{0:T(128)}, u32[]{:S(2)}) copy-start(s32[2]{0:T(128)} %constant.46) | copy-start | bytes 28
  361.4 47.8 %copy-start.4 = (s32[2]{0:T(128)S(1)}, s32[2]{0:T(128)}, u32[]{:S(2)}) copy-start(s32[2]{0:T(128)} %constant.49) | copy-start | bytes 28
  361.4 185.9 %all-reduce.8.cloned.1.call-start = ((), (), s32[]{:S(2)}) async-start(), calls=%async_computation.6 | async-start | bytes 4194304 | tf_op jit(solution)/shard_map/psum | solution.py:63
  408.9 138.4 %copy-start.6 = (f32[1024]{0:T(1024)S(1)}, f32[1024]{0:T(1024)}, u32[]{:S(2)}) copy-start(f32[1024]{0:T(1024)} %param.16) | copy-start | bytes 12292
  409.0 466.7 %reduce-scatter.2.cloned.1.call-start = ((), (), s32[]{:S(2)}) async-start(), calls=%async_computation.7 | async-start | bytes 4259840 | tf_op jit(solution)/shard_map/reduce_scatter | solution.py:70
Sparse Core Ops, SparseCore 0:
  9.8 50.2 all-gather.6
  61.9 46.7 all-gather.4
  110.5 46.6 all-gather.8
  159.9 45.9 all-reduce.9
  210.0 149.1 all-reduce.5
  361.5 40.8 all-gather.10
  409.1 62.8 all-reduce.7
  554.6 320.9 reduce-scatter.1
where the time goes:
time: 940 us
  waiting for transfers between devices  693 us (74%)
  local copies, waits for them, and re-layouts  138 us (15%)
  blocking collectives  63.2 us (7%)
  matrix products  25 us (3%)
  between operations  14.3 us (2%)
    reduce_scatter x1, waiting for transfers between devices, body(): lax.psum_scatter(jnp.dot(actives, dec_weight, preferred_element_type=jnp....  321 us
    psum x1, waiting for transfers between devices, body(): block_sum = lax.psum(down_terms, 'tensor')  149 us
    unnamed x18, local copies, waits for them, and re-layouts  137 us
    psum x1, blocking collectives, body(): lax.psum((jnp.sum(misfit * misfit, axis=1), jnp.sum(kept_f * kept_f, axis...  54.9 us
    psum x1, waiting for transfers between devices, body(): gate_pre, up_pre = lax.psum((gate_part, up_part), 'rep')  48.5 us
    all_gather x1, waiting for transfers between devices, body(): lax.all_gather(down_weight, 'dp', axis=2, tiled=True)[:, 0, :]  44.9 us
    all_gather x1, waiting for transfers between devices, body(): lax.all_gather(gate_weight, 'dp', axis=1, tiled=True)[0]  44.8 us
    all_gather x1, waiting for transfers between devices, body(): lax.all_gather(up_weight, 'dp', axis=1, tiled=True)[0]  41.2 us
  transfers between devices with their start and end apart: 8, of which 7 were waited for; matrix products, arithmetic and copies ran while one was open for 16% of the time, Pallas kernels for 0%

commit v1 on v0

--- a/solution.py
+++ b/solution.py
@@ -51,7 +51,7 @@
         preferred_element_type=jnp.float32,
     )
     rows_dev = tok_grp // n_tensor
-    block_sum = lax.psum(down_terms, "tensor")
+    block_sum = jnp.sum(jax.lax.all_gather(down_terms, axis_name="tensor"), 0)
     group_out = (resid_f + block_sum).astype(jnp.bfloat16)
     resid_rows = lax.dynamic_slice_in_dim(
         group_out, lax.axis_index("tensor") * rows_dev, rows_dev, 0

time: 940 us -> 1010 us (1.074)
  waiting for transfers between devices: 693 us -> 759 us
    all_gather x0 -> x1, waiting for transfers between devices: none -> 225 us  [body(): block_sum = jnp.sum(jax.lax.all_gather(down_terms, axis_name='tensor'), 0)]
    psum x1 -> x0, waiting for transfers between devices: 149 us -> none  [body(): block_sum = lax.psum(down_terms, 'tensor')]
    all_gather x1, waiting for transfers between devices: 41 us -> 30.7 us  [body(): slab_input = lax.all_gather(group_out, 'dp', axis=0, tiled=True)]
  transfers between devices with their start and end apart: 8 -> 8, of which waited for: 7 -> 7; matrix products, arithmetic and copies ran while one was open for 16% -> 15% of each run, Pallas kernels for 0% -> 0%
where the time goes in v1:
time: 1010 us
  waiting for transfers between devices  759 us (75%)
  local copies, waits for them, and re-layouts  138 us (14%)
  blocking collectives  62.7 us (6%)
  matrix products  25 us (2%)
  between operations  14.3 us (1%)
  other arithmetic  12 us (1%)
    reduce_scatter x1, waiting for transfers between devices, body(): lax.psum_scatter(jnp.dot(actives, dec_weight, preferred_element_type=jnp....  321 us
    all_gather x1, waiting for transfers between devices, body(): block_sum = jnp.sum(jax.lax.all_gather(down_terms, axis_name='tensor'), 0)  225 us
    unnamed x18, local copies, waits for them, and re-layouts  137 us
    psum x1, blocking collectives, body(): lax.psum((jnp.sum(misfit * misfit, axis=1), jnp.sum(kept_f * kept_f, axis...  54.5 us
    psum x1, waiting for transfers between devices, body(): gate_pre, up_pre = lax.psum((gate_part, up_part), 'rep')  48.5 us
    all_gather x1, waiting for transfers between devices, body(): lax.all_gather(down_weight, 'dp', axis=2, tiled=True)[:, 0, :]  44.9 us
    all_gather x1, waiting for transfers between devices, body(): lax.all_gather(gate_weight, 'dp', axis=1, tiled=True)[0]  44.8 us
    all_gather x1, waiting for transfers between devices, body(): lax.all_gather(up_weight, 'dp', axis=1, tiled=True)[0]  41.2 us
  transfers between devices with their start and end apart: 8, of which 7 were waited for; matrix products, arithmetic and copies ran while one was open for 15% of the time, Pallas kernels for 0%

profile of v1, /device:TPU:1, one launch (start us, length us, event | category | flops | bytes accessed | tf_op | source)
XLA Modules:
  0.0 1011.4 jit_solution(12396595572561924730)
XLA Ops:
  7.2 0.7 all-gather.9.cloned.1.call-update
  8.0 0.7 all-gather.7.cloned.1.call-update
  8.7 0.7 all-gather.11.cloned.1.call-update
  9.5 1.2 fusion.8
  10.7 8.3 psum.42
  18.9 41.2 %all-gather.9.cloned.1.call-done = bf16[1,2048,896]{2,1,0:T(8,128)(2,1)} async-done(((bf16[1,512,896]{2,1,0:T(8,128)(2,1)}), bf16[1,2048,896]{2,1,0:T(8,128)(2,1)}) %all-gather.9.cloned.1.call-update) | async-done | bytes 3670032 | tf_op jit(solution)/shard_map/all_gather | solution.py:43
  60.1 3.8 fusion.2
  63.9 44.8 %all-gather.7.cloned.1.call-done = bf16[1,2048,896]{2,1,0:T(8,128)(2,1)} async-done(((bf16[1,512,896]{2,1,0:T(8,128)(2,1)}), bf16[1,2048,896]{2,1,0:T(8,128)(2,1)}) %all-gather.7.cloned.1.call-update) | async-done | bytes 3670032 | tf_op jit(solution)/shard_map/all_gather | solution.py:38
  108.7 3.6 fusion.4
  112.4 44.9 %all-gather.11.cloned.1.call-done = bf16[896,1,2048]{2,0,1:T(8,128)(2,1)} async-done(((bf16[896,1,512]{2,0,1:T(8,128)(2,1)}), bf16[896,1,2048]{2,0,1:T(8,128)(2,1)}) %all-gather.11.cloned.1.call-update) | async-done | bytes 3670032 | tf_op jit(solution)/shard_map/all_gather | solution.py:50
  157.3 48.5 %all-reduce.7.cloned.1.call-done = (f32[128,896]{1,0:T(8,128)}, f32[128,896]{1,0:T(8,128)}) async-done(((f32[128,896]{1,0:T(8,128)}, f32[128,896]{1,0:T(8,128)}), (f32[128,896]{1,0:T(8,128)}, f32[128,896]{1,0:T(8,128)})) %all-reduce.7.cloned.1.call-update) | async-done | bytes 917520 | tf_op jit(solution)/shard_map/psum | solution.py:46
  205.8 4.1 fusion
  210.0 225.4 %all-gather.15.cloned.1.call-done = f32[2048,2048]{1,0:T(8,128)} async-done(((f32[128,2048]{1,0:T(8,128)}), f32[2048,2048]{1,0:T(8,128)}) %all-gather.15.cloned.1.call-update) | async-done | bytes 16777232 | tf_op jit(solution)/shard_map/all_gather | solution.py:54
  435.4 7.4 reduce_sum.37
  442.9 0.9 fusion.11
  443.9 30.7 %all-gather.13.cloned.1.call-done = bf16[512,2048]{1,0:T(8,128)(2,1)} async-done(((bf16[128,2048]{1,0:T(8,128)(2,1)}), bf16[512,2048]{1,0:T(8,128)(2,1)}) %all-gather.13.cloned.1.call-update) | async-done | bytes 2097168 | tf_op jit(solution)/shard_map/all_gather | solution.py:59
  474.6 6.5 fusion.6
  481.8 137.1 %scatter_custom_fusion = pred[524288]{0:T(1024)(128)(4,1)S(1)} fusion(s32[32768]{0:T(1024)S(1)} %reshape.26, pred[32768]{0:T(1024)(128)(4,1)S(1)} %broadcast.49, pred[]{:T(512)} %constant.14.clone.1), kind=kCustom, calls=%fused_computation.21 | custom fusion | bytes 524289
  618.9 0.6 reshape.25
  619.6 7.1 fusion.12
  626.7 321.2 %reduce-scatter.2.cloned.1.call-done = f32[8,2048]{1,0:T(8,128)} async-done(((f32[512,2048]{1,0:T(8,128)}), f32[8,2048]{1,0:T(8,128)}) %reduce-scatter.2.cloned.1.call-update) | async-done | bytes 65552 | tf_op jit(solution)/shard_map/reduce_scatter | solution.py:70
  947.9 1.6 fusion.23
  949.5 54.5 %all-reduce = (f32[8]{0:T(128)S(1)}, f32[8]{0:T(128)S(1)}) all-reduce(f32[8]{0:T(128)S(1)} %get-tuple-element.4, f32[8]{0:T(128)S(1)} %get-tuple-element.3), channel_id=1, replica_groups=mesh['dp'=4,'tensor'=16,'rep'=4] {'rep'}, use_global_device_ids=true, to_apply=%region_9.10 | all-reduce | flops 16 | bytes 128 | tf_op jit(solution)/shard_map/psum | solution.py:80
  1004.0 0.5 add_divide_fusion
  (37 shorter events, 1.0 us)
Async XLA Ops:
  7.2 53.0 %all-gather.9.cloned.1.call-start = ((), (), s32[]{:S(2)}) async-start(), calls=%async_computation.2 | async-start | bytes 4587520 | tf_op jit(solution)/shard_map/all_gather | solution.py:43
  7.9 100.8 %copy-start = (bf16[128,2048]{1,0:T(8,128)(2,1)S(1)}, bf16[128,2048]{1,0:T(8,128)(2,1)}, u32[]{:S(2)}) copy-start(bf16[128,2048]{1,0:T(8,128)(2,1)} %param.10) | copy-start | bytes 1572868
  7.9 100.8 %copy-start.2 = (f32[2048]{0:T(1024)S(1)}, f32[2048]{0:T(1024)}, u32[]{:S(2)}) copy-start(f32[2048]{0:T(1024)} %param.11) | copy-start | bytes 24580
  7.9 100.8 %all-gather.7.cloned.1.call-start = ((), (), s32[]{:S(2)}) async-start(), calls=%async_computation.1 | async-start | bytes 4587520 | tf_op jit(solution)/shard_map/all_gather | solution.py:38
  8.7 148.6 %all-gather.11.cloned.1.call-start = ((), (), s32[]{:S(2)}) async-start(), calls=%async_computation.3 | async-start | bytes 4587520 | tf_op jit(solution)/shard_map/all_gather | solution.py:50
  9.4 196.4 %all-reduce.7.cloned.1.call-start = ((), (), s32[]{:S(2)}) async-start(), calls=%async_computation.8 | async-start | bytes 1835008 | tf_op jit(solution)/shard_map/psum | solution.py:46
  112.3 323.1 %all-gather.15.cloned.1.call-start = ((), (), s32[]{:S(2)}) async-start(), calls=%async_computation.7 | async-start | bytes 17825792 | tf_op jit(solution)/shard_map/all_gather | solution.py:54
  209.9 264.7 %all-gather.13.cloned.1.call-start = ((), (), s32[]{:S(2)}) async-start(), calls=%async_computation.4 | async-start | bytes 2621440 | tf_op jit(solution)/shard_map/all_gather | solution.py:59
  435.4 39.2 %copy-start.3 = (f32[2048]{0:T(1024)S(1)}, f32[2048]{0:T(1024)}, u32[]{:S(2)}) copy-start(f32[2048]{0:T(1024)} %param.18) | copy-start | bytes 24580
  443.8 37.4 %copy-start.1 = (s32[512,64]{0,1:T(8,128)S(1)}, s32[512,64]{0,1:T(8,128)}, u32[]{:S(2)}) copy-start(s32[512,64]{0,1:T(8,128)} %param.19) | copy-start | bytes 393220
  443.8 37.5 %copy-start.5 = (s32[2]{0:T(128)S(1)}, s32[2]{0:T(128)}, u32[]{:S(2)}) copy-start(s32[2]{0:T(128)} %constant.46) | copy-start | bytes 28
  443.8 37.6 %copy-start.4 = (s32[2]{0:T(128)S(1)}, s32[2]{0:T(128)}, u32[]{:S(2)}) copy-start(s32[2]{0:T(128)} %constant.49) | copy-start | bytes 28
  443.8 175.7 %all-reduce.5.cloned.1.call-start = ((), (), s32[]{:S(2)}) async-start(), calls=%async_computation.5 | async-start | bytes 4194304 | tf_op jit(solution)/shard_map/psum | solution.py:63
  481.1 138.4 %copy-start.6 = (f32[1024]{0:T(1024)S(1)}, f32[1024]{0:T(1024)}, u32[]{:S(2)}) copy-start(f32[1024]{0:T(1024)} %param.16) | copy-start | bytes 12292
  481.2 466.7 %reduce-scatter.2.cloned.1.call-start = ((), (), s32[]{:S(2)}) async-start(), calls=%async_computation.6 | async-start | bytes 4259840 | tf_op jit(solution)/shard_map/reduce_scatter | solution.py:70
Sparse Core Ops, SparseCore 0:
  9.8 50.2 all-gather.8
  61.9 46.7 all-gather.6
  110.5 46.6 all-gather.10
  159.9 45.9 all-reduce.6
  210.0 225.3 all-gather.14
  443.9 30.6 all-gather.12
  481.3 62.8 all-reduce.4
  626.8 321.0 reduce-scatter.1
